TPU v7x, 32 devices: a whole 2x2x4 slice. The times are simulated.
32 devices in a mesh: groups: 2 (over y), inner: 4 (over z), outer: 4 (over x, core).
Axes of the slice: x: 2, y: 2, z: 4, core: 2. Of those that a mesh axis runs over, the one named last changes fastest.
Arguments:
- queries: bfloat16 [8192, 1024], P(('groups', 'outer', 'inner')), parts along dimension 0, may hold values from -6 to 6
- keys: bfloat16 [8192, 1024], P(('groups', 'outer', 'inner')), parts along dimension 0, may hold values from -6 to 6
- values: bfloat16 [8192, 1024], P(('groups', 'outer', 'inner')), parts along dimension 0, may hold values from -6 to 6
- retain: float32 [8192, 8], P(('groups', 'outer', 'inner')), parts along dimension 0, may hold values from 0.4 to 1
- step: float32 [8192, 8], P(('groups', 'outer', 'inner')), parts along dimension 0, may hold values from 0.000625 to 0.0125
- momentum: float32 [8192, 8], P(('groups', 'outer', 'inner')), parts along dimension 0, may hold values from 0.97 to 0.99
- init_memory: float32 [8, 128, 128], replicated, may hold values from -0.1875 to 0.1875
- init_momentum: float32 [8, 128, 128], replicated, may hold values from -0.1875 to 0.1875
Outputs:
- retrieved: bfloat16 [8192, 1024], P(('groups', 'outer', 'inner')), parts along dimension 0
There are 2 independent parts, one for each index of `groups`. A program takes and returns all parts, laid end to end along the dimension named above; an argument that names none is the same for every part. Nothing has to cross between parts.
All inputs are finite; a program needn't handle non-finite values.
Results may differ from a plain program's by a relative error of at most 0.001.
Values sent between devices are 32-bit elements; how exact they have to be, the bound alone decides.
No kernel may reach another device: no remote copies, remote signals or barrier semaphores. Data moves between devices by JAX's collectives and lax.ppermute only.
A program may use at most 256 MiB of HBM per device.

v0:
```python
import jax
import jax.numpy as jnp
from jax import lax
from jax.sharding import PartitionSpec as P


def carried_in(value, axis, join, neutral):
    count, mine = (lax.axis_size(axis), lax.axis_index(axis))
    pieces = jax.tree.map(lambda part: lax.all_gather(part, axis), value)
    total = jax.tree.map(
        lambda part, zero: jnp.full_like(part, 0) + jnp.asarray(zero, part.dtype), value, neutral
    )

    def turn(position, total):
        longer = join(total, jax.tree.map(lambda part: part[position], pieces))
        return jax.tree.map(lambda new, old: jnp.where(position < mine, new, old), longer, total)

    return lax.fori_loop(0, count - 1, turn, total)


def from_root(block, axis, owner):
    block = jnp.where(lax.axis_index(axis) == owner, block, jnp.zeros_like(block))
    return lax.psum(block, axis)


def unit_rows(source, heads):
    rows = source.astype(jnp.float32).reshape(source.shape[0], heads, -1)
    return rows * lax.rsqrt(jnp.sum(rows * rows, -1, keepdims=True) + 1e-06)


def block_terms(queries, keys, values, retain, step, momentum):
    length = queries.shape[0]
    heads = retain.shape[1]
    precise = lax.Precision.HIGHEST
    query_unit = unit_rows(queries, heads)
    key_unit = unit_rows(keys, heads)
    value_rows = values.astype(jnp.float32).reshape(length, heads, -1)
    key_width = key_unit.shape[2]
    log_retain = jnp.cumsum(jnp.log(retain), 0).T
    log_moment = jnp.cumsum(jnp.log(momentum), 0).T
    position = jnp.arange(length)
    causal = (position[:, None] >= position[None, :])[None]
    retain_decay = jnp.where(
        causal,
        jnp.exp(jnp.where(causal, log_retain[:, :, None] - log_retain[:, None, :], 0.0)),
        0.0,
    )
    momentum_decay = jnp.where(
        causal,
        jnp.exp(jnp.where(causal, log_moment[:, :, None] - log_moment[:, None, :], 0.0)),
        0.0,
    )
    weights = jnp.einsum("htu,hur->htr", retain_decay, momentum_decay, precision=precise)
    carry_scale = jnp.einsum("htu,hu->ht", retain_decay, jnp.exp(log_moment), precision=precise)
    scores = jnp.einsum("thd,rhd->htr", query_unit, key_unit, precision=precise)
    step_rows = step.T
    mixing = scores * weights * step_rows[:, None, :]
    memory_weight = weights[:, -1, :] * step_rows
    moment_weight = jnp.exp(log_moment[:, -1:] - log_moment) * step_rows
    memory_gram = jnp.einsum(
        "rhd,hr,rhe->hde", key_unit, memory_weight, key_unit, precision=precise
    )
    moment_gram = jnp.einsum(
        "rhd,hr,rhe->hde", key_unit, moment_weight, key_unit, precision=precise
    )
    identity = jnp.eye(key_width, dtype=jnp.float32)[None]
    retain_end = jnp.exp(log_retain[:, -1])[:, None, None]
    moment_end = jnp.exp(log_moment[:, -1])[:, None, None]
    carry_end = carry_scale[:, -1][:, None, None]
    upper_rows = jnp.concatenate([retain_end * identity - memory_gram, -moment_gram], axis=2)
    lower_rows = jnp.concatenate([carry_end * identity, moment_end * identity], axis=2)
    transition = jnp.concatenate([upper_rows, lower_rows], axis=1)
    memory_write = jnp.einsum(
        "rhd,hr,rhe->hde", value_rows, memory_weight, key_unit, precision=precise
    )
    moment_write = jnp.einsum(
        "rhd,hr,rhe->hde", value_rows, moment_weight, key_unit, precision=precise
    )
    offset = jnp.concatenate([memory_write, moment_write], axis=2)
    local_terms = (query_unit, key_unit, value_rows, jnp.exp(log_retain), carry_scale, mixing)
    return (transition, offset, local_terms)


def block_output(carried, local_terms):
    query_unit, key_unit, value_rows, retain_scale, carry_scale, mixing = local_terms
    precise = lax.Precision.HIGHEST
    key_width = query_unit.shape[2]
    memory = carried[:, :, :key_width]
    moment_part = carried[:, :, key_width:]
    residual = jnp.einsum("rhd,hed->hre", key_unit, memory, precision=precise) - jnp.transpose(
        value_rows, (1, 0, 2)
    )
    result = retain_scale[:, :, None] * jnp.einsum(
        "thd,hed->hte", query_unit, memory, precision=precise
    )
    result = result + carry_scale[:, :, None] * jnp.einsum(
        "thd,hed->hte", query_unit, moment_part, precision=precise
    )
    result = result - jnp.einsum("htr,hre->hte", mixing, residual, precision=precise)
    return jnp.transpose(result, (1, 0, 2)).reshape(query_unit.shape[0], -1).astype(jnp.bfloat16)


def advance_state(carried, transition, offset):
    return jnp.einsum("hij,hjk->hik", carried, transition, precision=lax.Precision.HIGHEST) + offset


def compose(earlier, later):
    joined = jnp.einsum("hij,hjk->hik", earlier[0], later[0], precision=lax.Precision.HIGHEST)
    return (joined, advance_state(earlier[1], later[0], later[1]))


def apply_earlier(gathered, first_state):
    my_group = lax.axis_index("outer")

    def advance_group(index, carried):
        moved = advance_state(carried, gathered[0][index], gathered[1][index])
        return jnp.where(index < my_group, moved, carried)

    return lax.fori_loop(0, gathered[0].shape[0], advance_group, first_state)


def local(queries, keys, values, retain, step, momentum, init_memory, init_momentum):
    transition, offset, local_terms = block_terms(queries, keys, values, retain, step, momentum)
    identity_maps = (
        jnp.broadcast_to(jnp.eye(transition.shape[1], dtype=jnp.float32), transition.shape),
        jnp.zeros_like(offset),
    )
    before = carried_in((transition, offset), "inner", compose, identity_maps)
    through = compose(before, (transition, offset))
    first_state = jnp.concatenate([init_memory, init_momentum], axis=2)
    last_inner = lax.axis_size("inner") - 1
    group_map = (
        from_root(through[0], "inner", last_inner),
        from_root(through[1], "inner", last_inner),
    )
    gathered = (
        lax.all_gather(group_map[0][None], "outer", axis=0, tiled=True),
        lax.all_gather(group_map[1][None], "outer", axis=0, tiled=True),
    )
    entry_state = apply_earlier(gathered, first_state)
    block_state = advance_state(entry_state, before[0], before[1])
    return block_output(block_state, local_terms)


def solution(mesh):
    placed = (
        P(("groups", "outer", "inner"), None),
        P(("groups", "outer", "inner"), None),
        P(("groups", "outer", "inner"), None),
        P(("groups", "outer", "inner"), None),
        P(("groups", "outer", "inner"), None),
        P(("groups", "outer", "inner"), None),
        P(),
        P(),
    )
    return jax.shard_map(
        local,
        mesh=mesh,
        in_specs=placed,
        out_specs=P(("groups", "outer", "inner"), None),
        check_vma=False,
    )
```

profile of v0, /device:TPU:0, one launch (start us, length us, event | category | flops | bytes accessed | tf_op | source)
XLA Modules:
  0.0 601.0 jit_solution(4477719836671399538)
XLA Ops:
  10.5 2.9 fusion.39
  16.8 1.5 copy.116
  18.3 2.1 broadcast_multiply_fusion.1
  21.2 1.6 copy.115
  22.7 2.0 copy.120
  24.8 1.7 convolution_bitcast_fusion.2
  29.2 2.6 copy.125
  32.2 2.3 fusion.44
  35.1 1.4 convolution_negate_fusion
  36.5 1.4 convolution_subtract_fusion.1
  38.9 1.8 copy.119
  41.4 74.1 %all-gather.13.cloned.1.call-done = f32[32,128,256]{2,1,0:T(8,128)} async-done(((f32[8,128,256]{2,1,0:T(8,128)}), f32[32,128,256]{2,1,0:T(8,128)}) %all-gather.13.cloned.1.call-update) | async-done | bytes 4194320 | tf_op jit(solution)/shard_map/all_gather | solution.py:9
  115.4 149.8 %all-gather.11.cloned.1.call-done = f32[32,256,256]{2,1,0:T(8,128)} async-done(((f32[8,256,256]{2,1,0:T(8,128)}), f32[32,256,256]{2,1,0:T(8,128)}) %all-gather.11.cloned.1.call-update) | async-done | bytes 8388624 | tf_op jit(solution)/shard_map/all_gather | solution.py:9
  265.4 49.7 %while.30 = (s32[]{:T(128)}, f32[8,256,256]{1,2,0:T(8,128)S(1)}, f32[8,128,256]{1,2,0:T(8,128)}, s32[]{:T(128)}, f32[4,8,256,256]{3,2,1,0:T(8,128)}, /*index=5*/f32[4,8,128,256]{3,2,1,0:T(8,128)}, s32[]{:T(128)}, s32[]{:T(128)}) while((s32[]{:T(128)}, f32[8,256,256]{1,2,0:T(8,128)S(1)}, f32[8,128,256]{1,2,0:T(8,128)}, s32[]{:T(128)}, ...), condition=%wide.region_7.8_spmd.clone, body=%wide.region_6.7_spmd.clone.sunk | while | flops 2417491968 | bytes 25168492 | solution.py:18
  265.4 2.3 constant_dynamic-slice_fusion.5
  267.7 1.5 copy.193
  270.5 6.1 %fusion.112 = f32[8,128,256]{1,2,0:T(8,128)} fusion(f32[4,8,256,256]{3,2,1,0:T(8,128)} %get-tuple-element.387, s32[]{:T(128)} %get-tuple-element.375, f32[1,8,128,256]{2,3,1,0:T(8,128)S(1)} %copy.193, f32[8,128,256]{1,2,0:T(8,128)S(1)} %copy.218, pred[]{:T(512)S(6)} %compare.3, pred[]{:T(512)S(6)} %lt.44), kind=kOutput, calls=%fused_computation.17.clone.1 | convolution fusion | flops 806354944 | bytes 6293504 | tf_op jit(solution)/shard_map/while/body/eval_jaxpr/hij,hjk->hik/dot_general | solution.py:104
  276.8 5.1 bitcast_select_fusion.2
  281.9 2.3 constant_dynamic-slice_fusion.5
  284.2 1.5 copy.193
  287.0 6.1 %fusion.112 = f32[8,128,256]{1,2,0:T(8,128)} fusion(f32[4,8,256,256]{3,2,1,0:T(8,128)} %get-tuple-element.387, s32[]{:T(128)} %get-tuple-element.375, f32[1,8,128,256]{2,3,1,0:T(8,128)S(1)} %copy.193, f32[8,128,256]{1,2,0:T(8,128)S(1)} %copy.218, pred[]{:T(512)S(6)} %compare.3, pred[]{:T(512)S(6)} %lt.44), kind=kOutput, calls=%fused_computation.17.clone.1 | convolution fusion | flops 806354944 | bytes 6293504 | tf_op jit(solution)/shard_map/while/body/eval_jaxpr/hij,hjk->hik/dot_general | solution.py:104
  293.3 5.1 bitcast_select_fusion.2
  298.4 2.3 constant_dynamic-slice_fusion.5
  300.7 1.5 copy.193
  303.5 6.1 %fusion.112 = f32[8,128,256]{1,2,0:T(8,128)} fusion(f32[4,8,256,256]{3,2,1,0:T(8,128)} %get-tuple-element.387, s32[]{:T(128)} %get-tuple-element.375, f32[1,8,128,256]{2,3,1,0:T(8,128)S(1)} %copy.193, f32[8,128,256]{1,2,0:T(8,128)S(1)} %copy.218, pred[]{:T(512)S(6)} %compare.3, pred[]{:T(512)S(6)} %lt.44), kind=kOutput, calls=%fused_computation.17.clone.1 | convolution fusion | flops 806354944 | bytes 6293504 | tf_op jit(solution)/shard_map/while/body/eval_jaxpr/hij,hjk->hik/dot_general | solution.py:104
  309.8 5.1 bitcast_select_fusion.2
  315.1 5.2 fusion.49
  320.3 4.8 select_bitcast_fusion
  325.2 119.8 %all-reduce.3.cloned.1.call-done = (f32[1,8,256,256]{3,2,1,0:T(8,128)}, f32[1,8,128,256]{2,3,1,0:T(8,128)}) async-done(((f32[1,8,256,256]{3,2,1,0:T(8,128)}, f32[1,8,128,256]{2,3,1,0:T(8,128)}), (f32[1,8,256,256]{3,2,1,0:T(8,128)}, f32[1,8,128,256]{2,3,1,0:T(8,128)})) %all-reduce.3.cloned.1.call-update) | async-done | bytes 3145744 | tf_op jit(solution)/shard_map/psum | solution.py:23
  445.0 2.5 copy.133
  452.1 5.1 fusion.66
  457.2 1.3 copy.138
  458.5 22.6 %all-gather.9.cloned.1.call-done = f32[4,8,128,256]{3,2,1,0:T(8,128)} async-done(((f32[1,8,128,256]{3,2,1,0:T(8,128)}), f32[4,8,128,256]{3,2,1,0:T(8,128)}) %all-gather.9.cloned.1.call-update) | async-done | bytes 4194320 | tf_op jit(solution)/shard_map/all_gather | solution.py:138
  481.2 59.7 %all-gather.7.cloned.1.call-done = f32[4,8,256,256]{3,2,1,0:T(8,128)} async-done(((f32[1,8,256,256]{3,2,1,0:T(8,128)}), f32[4,8,256,256]{3,2,1,0:T(8,128)}) %all-gather.7.cloned.1.call-update) | async-done | bytes 8388624 | tf_op jit(solution)/shard_map/all_gather | solution.py:137
  540.9 41.4 %while.29 = (s32[]{:T(128)}, f32[8,128,256]{1,2,0:T(8,128)}, s32[]{:T(128)}, f32[4,8,256,256]{3,2,1,0:T(8,128)}, f32[4,8,128,256]{3,2,1,0:T(8,128)}, /*index=5*/s32[]{:T(128)}) while((s32[]{:T(128)}, f32[8,128,256]{1,2,0:T(8,128)}, s32[]{:T(128)}, f32[4,8,256,256]{3,2,1,0:T(8,128)}, f32[4,8,128,256]{3,2,1,0:T(8,128)}, ...), condition=%wide.region_11.12_spmd, body=%wide.region_10.11_spmd.sunk | while | flops 805830656 | bytes 16777840 | solution.py:119
  541.1 1.3 constant_dynamic-slice_fusion.4
  542.4 1.3 copy.192
  545.3 6.1 %fusion.107 = f32[8,128,256]{1,2,0:T(8,128)} fusion(f32[8,128,256]{1,2,0:T(8,128)S(1)} %copy.216, f32[4,8,256,256]{3,2,1,0:T(8,128)} %get-tuple-element.406, s32[]{:T(128)} %get-tuple-element.397, f32[1,8,128,256]{2,3,1,0:T(8,128)S(1)} %copy-done, pred[]{:T(512)S(6)} %lt.43), kind=kOutput, calls=%fused_computation.5.clone.1 | convolution fusion | flops 805830656 | bytes 6291969 | tf_op jit(solution)/shard_map/while/body/eval_jaxpr/hij,hjk->hik/dot_general | solution.py:104
  551.4 1.3 constant_dynamic-slice_fusion.4
  552.7 1.3 copy.192
  555.6 6.1 %fusion.107 = f32[8,128,256]{1,2,0:T(8,128)} fusion(f32[8,128,256]{1,2,0:T(8,128)S(1)} %copy.216, f32[4,8,256,256]{3,2,1,0:T(8,128)} %get-tuple-element.406, s32[]{:T(128)} %get-tuple-element.397, f32[1,8,128,256]{2,3,1,0:T(8,128)S(1)} %copy-done, pred[]{:T(512)S(6)} %lt.43), kind=kOutput, calls=%fused_computation.5.clone.1 | convolution fusion | flops 805830656 | bytes 6291969 | tf_op jit(solution)/shard_map/while/body/eval_jaxpr/hij,hjk->hik/dot_general | solution.py:104
  563.0 1.3 copy.192
  565.9 6.1 %fusion.107 = f32[8,128,256]{1,2,0:T(8,128)} fusion(f32[8,128,256]{1,2,0:T(8,128)S(1)} %copy.216, f32[4,8,256,256]{3,2,1,0:T(8,128)} %get-tuple-element.406, s32[]{:T(128)} %get-tuple-element.397, f32[1,8,128,256]{2,3,1,0:T(8,128)S(1)} %copy-done, pred[]{:T(512)S(6)} %lt.43), kind=kOutput, calls=%fused_computation.5.clone.1 | convolution fusion | flops 805830656 | bytes 6291969 | tf_op jit(solution)/shard_map/while/body/eval_jaxpr/hij,hjk->hik/dot_general | solution.py:104
  572.0 1.3 constant_dynamic-slice_fusion.4
  573.3 1.3 copy.192
  576.2 6.1 %fusion.107 = f32[8,128,256]{1,2,0:T(8,128)} fusion(f32[8,128,256]{1,2,0:T(8,128)S(1)} %copy.216, f32[4,8,256,256]{3,2,1,0:T(8,128)} %get-tuple-element.406, s32[]{:T(128)} %get-tuple-element.397, f32[1,8,128,256]{2,3,1,0:T(8,128)S(1)} %copy-done, pred[]{:T(512)S(6)} %lt.43), kind=kOutput, calls=%fused_computation.5.clone.1 | convolution fusion | flops 805830656 | bytes 6291969 | tf_op jit(solution)/shard_map/while/body/eval_jaxpr/hij,hjk->hik/dot_general | solution.py:104
  582.3 4.0 convolution_add_fusion
  589.4 2.5 fusion.45
  (141 shorter events, 34.6 us)
Async XLA Ops:
  6.5 108.9 %all-gather.13.cloned.1.call-start = ((), (), s32[]{:S(2)}) async-start(), calls=%async_computation.3 | async-start | bytes 5242880 | tf_op jit(solution)/shard_map/all_gather | solution.py:9
  6.6 6.9 %copy-start.25 = (pred[256,256]{1,0:T(8,128)(4,1)}, pred[256,256]{1,0:T(8,128)(4,1)S(1)}, u32[]{:S(2)}) copy-start(pred[256,256]{1,0:T(8,128)(4,1)S(1)} %iota_compare_fusion) | copy-start | bytes 196612
  8.2 5.3 copy-start.28
  10.5 3.0 copy-start.31
  10.5 3.0 copy-start.27
  10.5 4.4 copy-start.21
  13.5 1.3 copy-start.16
  15.1 1.0 copy-start.22
  18.3 2.1 copy-start.23
  20.4 16.1 %copy-start.2 = (f32[256,8,128]{2,1,0:T(8,128)}, f32[256,8,128]{2,1,0:T(8,128)S(1)}, u32[]{:S(2)}) copy-start(f32[256,8,128]{2,1,0:T(8,128)S(1)} %get-tuple-element.291) | copy-start | bytes 3145732
  24.8 1.7 copy-start.6
  26.5 0.8 copy-start.19
  27.3 0.8 copy-start.20
  29.2 3.0 copy-start.32
  29.2 3.0 copy-start.26
  29.2 3.0 copy-start.29
  29.2 3.0 copy-start.30
  31.8 233.4 %all-gather.11.cloned.1.call-start = ((), (), s32[]{:S(2)}) async-start(), calls=%async_computation.2 | async-start | bytes 10485760 | tf_op jit(solution)/shard_map/all_gather | solution.py:9
  35.1 2.9 copy-start.8
  35.1 2.9 copy-start.10
  36.5 1.5 copy-start.12
  38.0 0.8 copy-start.14
  40.7 404.2 %all-reduce.3.cloned.1.call-start = ((), (), s32[]{:S(2)}) async-start(), calls=%async_computation.4 | async-start | bytes 6291456 | tf_op jit(solution)/shard_map/psum | solution.py:23
  315.1 5.2 copy-start.9
  315.1 5.2 copy-start.11
  315.1 5.2 copy-start.13
  315.1 5.2 copy-start.15
  325.2 156.0 %all-gather.9.cloned.1.call-start = ((), (), s32[]{:S(2)}) async-start(), calls=%async_computation.1 | async-start | bytes 5242880 | tf_op jit(solution)/shard_map/all_gather | solution.py:138
  447.5 1.0 copy-start.7
  447.5 2.0 copy-start.24
  447.5 93.4 %all-gather.7.cloned.1.call-start = ((), (), s32[]{:S(2)}) async-start(), calls=%async_computation | async-start | bytes 10485760 | tf_op jit(solution)/shard_map/all_gather | solution.py:137
  452.1 5.1 copy-start.1
  543.8 1.5 copy-start
  554.1 1.5 copy-start
  564.4 1.5 copy-start
  574.7 1.5 copy-start
  582.3 4.0 copy-start.4
  586.3 1.3 copy-start.3
  586.3 1.3 copy-start.18
  586.3 2.5 copy-start.17
  587.6 1.7 copy-start.5
Sparse Core Ops, SparseCore 0:
  31.9 83.4 all-gather.12
  117.0 148.1 all-gather.10
  325.3 119.6 all-reduce.2
  447.7 33.4 all-gather.8
  482.6 58.2 all-gather.6
where the time goes:
time: 609 us; the launch traced here: 601 us
  waiting for transfers between devices  427 us (70%)
  matrix products  93.8 us (15%)
  local copies, waits for them, and re-layouts  56.5 us (9%)
  between operations  13.9 us (2%)
  other arithmetic  8.6 us (1%)
    all_gather x2, waiting for transfers between devices, carried_in(): pieces = jax.tree.map(lambda part: lax.all_gather(part, axis), value)  224 us
    psum x1, waiting for transfers between devices, from_root(): return lax.psum(block, axis)  120 us
    all_gather x1, waiting for transfers between devices, local(): lax.all_gather(group_map[0][None], 'outer', axis=0, tiled=True)  59.7 us
    dot_general x9, matrix products, advance_state(): jnp.einsum('hij,hjk->hik', carried, transition, precision=lax.Precision.H...  51.8 us
    all_gather x1, waiting for transfers between devices, local(): lax.all_gather(group_map[1][None], 'outer', axis=0, tiled=True)  22.6 us
    dot_general x4, matrix products, compose(): jnp.einsum('hij,hjk->hik', earlier[0], later[0], precision=lax.Precision....  20.2 us
  transfers between devices with their start and end apart: 5, of which 5 were waited for; matrix products, arithmetic and copies ran while one was open for 3% of the time, Pallas kernels for 0%

commit v1 on v0

--- a/solution.py
+++ b/solution.py
@@ -2,6 +2,18 @@
 import jax.numpy as jnp
 from jax import lax
 from jax.sharding import PartitionSpec as P
+
+
+def gather_by_bits(array, axis, dim):
+    ways, here = (lax.axis_size(axis), lax.axis_index(axis))
+    grown, reach = (array, 1)
+    while reach < ways:
+        theirs = lax.ppermute(grown, axis, [(d, d ^ reach) for d in range(ways)])
+        mine_first = jnp.concatenate([grown, theirs], axis=dim)
+        theirs_first = jnp.concatenate([theirs, grown], axis=dim)
+        grown = jnp.where(here & reach == 0, mine_first, theirs_first)
+        reach = 2 * reach
+    return grown
 
 
 def carried_in(value, axis, join, neutral):
@@ -134,7 +146,7 @@
         from_root(through[1], "inner", last_inner),
     )
     gathered = (
-        lax.all_gather(group_map[0][None], "outer", axis=0, tiled=True),
+        gather_by_bits(group_map[0][None], "outer", 0),
         lax.all_gather(group_map[1][None], "outer", axis=0, tiled=True),
     )
     entry_state = apply_earlier(gathered, first_state)

time: 609 us -> 647 us (1.062)
  waiting for transfers between devices: 427 us -> 448 us
  other arithmetic: 8.6 us -> 24.4 us
    ppermute x0 -> x2, waiting for transfers between devices: none -> 105 us  [gather_by_bits(): theirs = lax.ppermute(grown, axis, [(d, d ^ reach) for d in range(ways)])]
    all_gather x1 -> x0, waiting for transfers between devices: 59.7 us -> none  [local(): lax.all_gather(group_map[0][None], 'outer', axis=0, tiled=True)]
    all_gather x1, waiting for transfers between devices: 22.6 us -> 0.01 us  [local(): lax.all_gather(group_map[1][None], 'outer', axis=0, tiled=True)]
    select_n x0 -> x2, other arithmetic: none -> 16.4 us  [gather_by_bits(): grown = jnp.where(here & reach == 0, mine_first, theirs_first)]
  transfers between devices with their start and end apart: 5 -> 6, of which waited for: 5 -> 5; matrix products, arithmetic and copies ran while one was open for 3% -> 6% of each run, Pallas kernels for 0% -> 0%
where the time goes in v1:
time: 647 us; the launch traced here: 639 us
  waiting for transfers between devices  448 us (69%)
  matrix products  93.8 us (14%)
  local copies, waits for them, and re-layouts  56.1 us (9%)
  other arithmetic  24.4 us (4%)
  between operations  14 us (2%)
    all_gather x2, waiting for transfers between devices, carried_in(): pieces = jax.tree.map(lambda part: lax.all_gather(part, axis), value)  224 us
    psum x1, waiting for transfers between devices, from_root(): return lax.psum(block, axis)  120 us
    ppermute x2, waiting for transfers between devices, gather_by_bits(): theirs = lax.ppermute(grown, axis, [(d, d ^ reach) for d in range(ways)])  105 us
    dot_general x9, matrix products, advance_state(): jnp.einsum('hij,hjk->hik', carried, transition, precision=lax.Precision.H...  51.9 us
    dot_general x4, matrix products, compose(): jnp.einsum('hij,hjk->hik', earlier[0], later[0], precision=lax.Precision....  20.2 us
    select_n x2, other arithmetic, gather_by_bits(): grown = jnp.where(here & reach == 0, mine_first, theirs_first)  16.4 us
  transfers between devices with their start and end apart: 6, of which 5 were waited for; matrix products, arithmetic and copies ran while one was open for 6% of the time, Pallas kernels for 0%

profile of v1, /device:TPU:0, one launch (start us, length us, event | category | flops | bytes accessed | tf_op | source)
XLA Modules:
  0.0 639.3 jit_solution(9182630735441655606)
XLA Ops:
  10.5 2.9 fusion.39
  13.5 1.3 copy-done.16
  17.7 2.1 broadcast_multiply_fusion.1
  20.6 1.6 copy.115
  22.1 2.0 copy.120
  24.2 1.7 convolution_bitcast_fusion.2
  28.7 2.6 copy.125
  31.6 2.3 fusion.44
  34.5 1.4 convolution_negate_fusion
  35.9 1.4 convolution_subtract_fusion.1
  38.3 1.8 copy.119
  40.8 74.1 %all-gather.10.cloned.1.call-done = f32[32,128,256]{2,1,0:T(8,128)} async-done(((f32[8,128,256]{2,1,0:T(8,128)}), f32[32,128,256]{2,1,0:T(8,128)}) %all-gather.10.cloned.1.call-update) | async-done | bytes 4194320 | tf_op jit(solution)/shard_map/all_gather | solution.py:21
  114.9 149.8 %all-gather.8.cloned.1.call-done = f32[32,256,256]{2,1,0:T(8,128)} async-done(((f32[8,256,256]{2,1,0:T(8,128)}), f32[32,256,256]{2,1,0:T(8,128)}) %all-gather.8.cloned.1.call-update) | async-done | bytes 8388624 | tf_op jit(solution)/shard_map/all_gather | solution.py:21
  264.8 49.5 %while.30 = (s32[]{:T(128)}, f32[8,256,256]{1,2,0:T(8,128)S(1)}, f32[8,128,256]{1,2,0:T(8,128)}, s32[]{:T(128)}, f32[4,8,256,256]{3,2,1,0:T(8,128)}, /*index=5*/f32[4,8,128,256]{3,2,1,0:T(8,128)}, s32[]{:T(128)}, s32[]{:T(128)}) while((s32[]{:T(128)}, f32[8,256,256]{1,2,0:T(8,128)S(1)}, f32[8,128,256]{1,2,0:T(8,128)}, s32[]{:T(128)}, ...), condition=%wide.region_7.8_spmd.clone, body=%wide.region_6.7_spmd.clone.sunk | while | flops 2417491968 | bytes 25168492 | solution.py:30
  264.8 2.3 constant_dynamic-slice_fusion.5
  267.1 1.5 copy.193
  269.9 6.1 fusion.112
  276.1 5.1 bitcast_select_fusion.2
  281.3 2.3 constant_dynamic-slice_fusion.5
  283.6 1.5 copy.193
  286.3 6.1 fusion.112
  292.6 5.1 bitcast_select_fusion.2
  297.7 2.3 constant_dynamic-slice_fusion.5
  300.0 1.5 copy.193
  302.8 6.1 fusion.112
  309.0 5.1 bitcast_select_fusion.2
  314.4 5.2 fusion.49
  319.5 4.8 select_bitcast_fusion
  324.4 119.8 %all-reduce.3.cloned.1.call-done = (f32[1,8,256,256]{3,2,1,0:T(8,128)}, f32[1,8,128,256]{2,3,1,0:T(8,128)}) async-done(((f32[1,8,256,256]{3,2,1,0:T(8,128)}, f32[1,8,128,256]{2,3,1,0:T(8,128)}), (f32[1,8,256,256]{3,2,1,0:T(8,128)}, f32[1,8,128,256]{2,3,1,0:T(8,128)})) %all-reduce.3.cloned.1.call-update) | async-done | bytes 3145744 | tf_op jit(solution)/shard_map/psum | solution.py:35
  444.2 2.6 copy.133
  446.8 1.9 collective-permute-done
  448.7 6.2 maximum_select_fusion.1
  459.8 5.0 fusion.66
  466.1 102.9 %collective-permute-done.1 = f32[2,8,256,256]{3,2,1,0:T(8,128)} collective-permute-done((f32[2,8,256,256]{3,2,1,0:T(8,128)}, f32[2,8,256,256]{3,2,1,0:T(8,128)}, u32[]{:S(2)}, u32[]{:S(2)}) %collective-permute-start.1) | collective-permute-done | bytes 4194336 | tf_op jit(solution)/shard_map/ppermute | solution.py:11
  568.9 10.2 %maximum_select_fusion = f32[4,8,256,256]{3,2,1,0:T(8,128)} fusion(f32[2,8,256,256]{3,2,1,0:T(8,128)} %collective-permute-done.1, f32[2,8,256,256]{3,2,1,0:T(8,128)} %maximum_select_fusion.1, pred[]{:T(512)S(6)} %eq.24), kind=kLoop, calls=%fused_computation.25 | loop fusion | flops 6291456 | bytes 16777216 | tf_op jit(solution)/shard_map/jit(_where)/select_n | solution.py:14
  579.2 41.4 %while.29 = (s32[]{:T(128)}, f32[8,128,256]{1,2,0:T(8,128)}, s32[]{:T(128)}, f32[4,8,256,256]{3,2,1,0:T(8,128)}, f32[4,8,128,256]{3,2,1,0:T(8,128)}, /*index=5*/s32[]{:T(128)}) while((s32[]{:T(128)}, f32[8,128,256]{1,2,0:T(8,128)}, s32[]{:T(128)}, f32[4,8,256,256]{3,2,1,0:T(8,128)}, f32[4,8,128,256]{3,2,1,0:T(8,128)}, ...), condition=%wide.region_11.12_spmd, body=%wide.region_10.11_spmd.sunk | while | flops 805830656 | bytes 16777840 | solution.py:131
  579.2 1.3 constant_dynamic-slice_fusion.4
  580.5 1.3 copy.192
  583.4 6.1 fusion.107
  589.5 1.3 constant_dynamic-slice_fusion.4
  590.9 1.3 copy.192
  593.7 6.1 fusion.107
  601.2 1.3 copy.192
  604.1 6.1 fusion.107
  611.5 1.3 copy.192
  614.4 6.1 fusion.107
  620.6 4.0 convolution_add_fusion
  627.6 2.6 fusion.45
  (144 shorter events, 37.3 us)
Async XLA Ops:
  6.5 108.3 %all-gather.10.cloned.1.call-start = ((), (), s32[]{:S(2)}) async-start(), calls=%async_computation.2 | async-start | bytes 5242880 | tf_op jit(solution)/shard_map/all_gather | solution.py:21
  6.6 6.9 %copy-start.25 = (pred[256,256]{1,0:T(8,128)(4,1)}, pred[256,256]{1,0:T(8,128)(4,1)S(1)}, u32[]{:S(2)}) copy-start(pred[256,256]{1,0:T(8,128)(4,1)S(1)} %iota_compare_fusion) | copy-start | bytes 196612
  8.2 5.3 copy-start.28
  10.5 4.3 copy-start.31
  10.5 4.3 copy-start.27
  10.5 4.6 copy-start.21
  13.5 1.3 copy-start.16
  15.2 1.0 copy-start.22
  17.7 2.1 copy-start.23
  19.8 16.1 %copy-start.2 = (f32[256,8,128]{2,1,0:T(8,128)}, f32[256,8,128]{2,1,0:T(8,128)S(1)}, u32[]{:S(2)}) copy-start(f32[256,8,128]{2,1,0:T(8,128)S(1)} %get-tuple-element.291) | copy-start | bytes 3145732
  24.2 1.7 copy-start.6
  25.9 0.8 copy-start.19
  26.7 0.8 copy-start.20
  28.7 2.9 copy-start.32
  28.7 3.0 copy-start.26
  28.7 3.0 copy-start.29
  28.7 3.0 copy-start.30
  31.3 233.4 %all-gather.8.cloned.1.call-start = ((), (), s32[]{:S(2)}) async-start(), calls=%async_computation.1 | async-start | bytes 10485760 | tf_op jit(solution)/shard_map/all_gather | solution.py:21
  34.5 2.9 copy-start.8
  34.5 2.9 copy-start.10
  35.9 1.5 copy-start.12
  37.4 0.8 copy-start.14
  40.2 404.0 %all-reduce.3.cloned.1.call-start = ((), (), s32[]{:S(2)}) async-start(), calls=%async_computation.3 | async-start | bytes 6291456 | tf_op jit(solution)/shard_map/psum | solution.py:35
  314.3 5.2 copy-start.9
  314.3 5.2 copy-start.11
  314.4 5.2 copy-start.13
  314.4 5.2 copy-start.15
  324.4 254.8 %all-gather.6.cloned.1.call-start = ((), (), s32[]{:S(2)}) async-start(), calls=%async_computation | async-start | bytes 5242880 | tf_op jit(solution)/shard_map/all_gather | solution.py:150
  444.2 4.5 collective-permute-start
  446.8 9.4 %copy-start.7 = (bf16[256,1024]{0,1:T(8,128)(2,1)S(1)}, bf16[256,1024]{0,1:T(8,128)(2,1)}, u32[]{:S(2)}) copy-start(bf16[256,1024]{0,1:T(8,128)(2,1)} %copy.120) | copy-start | bytes 1572868
  446.8 10.4 %copy-start.24 = (f32[8,128,128]{2,1,0:T(8,128)S(1)}, f32[8,128,128]{2,1,0:T(8,128)}, u32[]{:S(2)}) copy-start(f32[8,128,128]{2,1,0:T(8,128)} %param.18) | copy-start | bytes 1572868
  454.9 114.0 %collective-permute-start.1 = (f32[2,8,256,256]{3,2,1,0:T(8,128)}, f32[2,8,256,256]{3,2,1,0:T(8,128)}, u32[]{:S(2)}, u32[]{:S(2)}) collective-permute-start(f32[2,8,256,256]{3,2,1,0:T(8,128)} %maximum_select_fusion.1), channel_id=1, source_target_pairs={{0,2},{1,3},{2,0},{3,1},{4,6},{5,7},{6,4},{7,5},{8,10},{9,11},{10,... | collective-permute-start | bytes 12582920 | tf_op jit(solution)/shard_map/ppermute | solution.py:11
  459.7 5.0 copy-start.1
  581.8 1.5 copy-start
  592.2 1.5 copy-start
  602.5 1.5 copy-start
  612.9 1.5 copy-start
  620.6 4.0 copy-start.4
  624.5 1.3 copy-start.3
  624.5 1.3 copy-start.18
  624.6 2.5 copy-start.17
  625.9 1.7 copy-start.5
Sparse Core Ops, SparseCore 0:
  31.4 83.4 all-gather.9
  116.4 148.1 all-gather.7
  324.5 119.6 all-reduce.2
  446.9 54.9 all-gather.5
